TPU v7x, 256 devices: a whole 4x4x8 slice. The times are simulated.
256 devices in a mesh: req: 64 (over x, z, y_lo), kv: 4 (over y_hi, core).
Axes of the slice: x: 4, y: 4 (y_hi: 2, y_lo: 2; y = y_hi * 2 + y_lo), z: 8, core: 2. Of those that a mesh axis runs over, the one named last changes fastest.
Arguments:
- hidden: bfloat16 [64, 1024, 1536], P('req', 'kv'), may hold values from -6 to 6
- lengths: int32 [64], P('req'), may hold values from 1 to 2048, as said below
- key_cache: bfloat16 [64, 2048, 768], P('req', 'kv'), may hold values from -180 to 180
- value_cache: bfloat16 [64, 2048, 768], P('req', 'kv'), may hold values from -6 to 6
- norm_gain: bfloat16 [1536], replicated, may hold values from 0.099609375 to 1.8984375
- w_query: bfloat16 [1536, 1536], P('req', 'kv'), may hold values from -0.15625 to 0.15625
- w_key: bfloat16 [1536, 768], P('req', 'kv'), may hold values from -0.15625 to 0.15625
- w_value: bfloat16 [1536, 768], P('req', 'kv'), may hold values from -0.15625 to 0.15625
- w_out: bfloat16 [1536, 1536], P('req', 'kv'), may hold values from -0.15625 to 0.15625
Outputs:
- attended: bfloat16 [64, 1024, 1536], P('req', 'kv')
- new_keys: bfloat16 [64, 1024, 768], P('req', 'kv')
- new_values: bfloat16 [64, 1024, 768], P('req', 'kv')
Inputs may be any that keep to these rules, and one draw needn't show every extreme that they name: `lengths`: at least a quarter of the requests (one or more) hold more than 1792 tokens, one of them exactly 2048; the others hold fewer than 512.
All inputs are finite; a program needn't handle non-finite values.
Results may differ from a plain program's by a relative error of at most 0.011.
Values may be sent and summed in bfloat16 or wider, within the bound.
A program may use at most 192 MiB of HBM per device.

v0:
```python
import jax
import jax.numpy as jnp
from jax import lax
from jax.sharding import PartitionSpec as P

H = 16
KVH = 8
HD = 96
rope_base = 100000.0
masked_score = -1e30


def rms_norm(states, gain):
    mean_square = jnp.mean(states * states, axis=-1, keepdims=True)
    scaled = states * lax.rsqrt(mean_square + 1e-05) * gain.astype(jnp.float32)
    return scaled.astype(jnp.bfloat16)


def rotate(values, positions):
    count = values.shape[0]
    heads = values.shape[1] // HD
    half = HD // 2
    frequency = rope_base ** (-(jnp.arange(half, dtype=jnp.float32) * 2.0 / HD))
    angle = positions[:, None] * frequency[None, :]
    cosine = jnp.cos(angle)[:, None, :]
    sine = jnp.sin(angle)[:, None, :]
    shaped = values.reshape(count, heads, HD)
    first = shaped[..., :half]
    second = shaped[..., half:]
    turned = jnp.concatenate(
        [first * cosine - second * sine, second * cosine + first * sine], axis=-1
    )
    return turned.reshape(count, heads * HD)


def fold_three(inputs, pieces):
    return tuple((jnp.dot(inputs, piece, preferred_element_type=jnp.float32) for piece in pieces))


def fold_single(inputs, piece):
    return jnp.dot(inputs, piece, preferred_element_type=jnp.float32)


def combine_blocks(blocks, share):
    block_count = blocks.shape[0]
    count = blocks.shape[1]
    numerator = jnp.zeros((count, H, HD), jnp.float32)
    for block in range(block_count):
        weight_rows = jnp.transpose(share[block])[:, :, None]
        numerator = (
            numerator + blocks[block].reshape(count, H, HD).astype(jnp.float32) * weight_rows
        )
    denominator = jnp.transpose(jnp.sum(share, axis=0))[:, :, None]
    return (numerator / denominator).reshape(count, H * HD).astype(jnp.bfloat16)


def body(hidden, lengths, key_cache, value_cache, norm_gain, w_query, w_key, w_value, w_out):
    rows_here = hidden.shape[1]
    width = hidden.shape[2]
    kv_count = lax.axis_size("kv")
    kv_index = lax.axis_index("kv")
    appended = rows_here * kv_count
    slots = key_cache.shape[1]
    groups = H // KVH
    scale = HD ** (-0.5)
    length = lengths[0]
    normed = rms_norm(hidden[0].astype(jnp.float32), norm_gain)
    query_cols, key_cols, value_cols = (
        lax.all_gather(w_query, "kv", axis=1, tiled=True),
        lax.all_gather(w_key, "kv", axis=1, tiled=True),
        lax.all_gather(w_value, "kv", axis=1, tiled=True),
    )
    proj_query, proj_key, proj_value = fold_three(
        normed,
        (
            lax.all_gather(query_cols, "req", axis=0, tiled=True),
            lax.all_gather(key_cols, "req", axis=0, tiled=True),
            lax.all_gather(value_cols, "req", axis=0, tiled=True),
        ),
    )
    positions = (length + kv_index * rows_here + jnp.arange(rows_here, dtype=jnp.int32)).astype(
        jnp.float32
    )
    queries_here = rotate(proj_query, positions).astype(jnp.bfloat16)
    new_keys = rotate(proj_key, positions).astype(jnp.bfloat16)
    new_values = proj_value.astype(jnp.bfloat16)
    queries = lax.all_gather(queries_here, "kv", axis=0, tiled=True)
    keys_all = jnp.concatenate([key_cache[0], new_keys], axis=0)
    values_all = jnp.concatenate([value_cache[0], new_values], axis=0)
    key_count = keys_all.shape[0]
    query_index = jnp.arange(appended, dtype=jnp.int32)
    cache_live = kv_index * slots + jnp.arange(slots, dtype=jnp.int32) < length
    own_index = kv_index * rows_here + jnp.arange(rows_here, dtype=jnp.int32)
    visible = jnp.concatenate(
        [
            jnp.broadcast_to(cache_live[None, :], (appended, slots)),
            own_index[None, :] <= query_index[:, None],
        ],
        axis=1,
    )
    query_heads = jnp.transpose(queries.reshape(appended, KVH, groups, HD), (1, 0, 2, 3))
    key_heads = jnp.transpose(keys_all.reshape(key_count, KVH, HD), (1, 0, 2))
    value_heads = jnp.transpose(values_all.reshape(key_count, KVH, HD), (1, 0, 2))

    def attend(operands):
        query_block, key_block, value_block = operands
        score = (
            jnp.einsum("qgd,kd->gqk", query_block, key_block, preferred_element_type=jnp.float32)
            * scale
        )
        score = jnp.where(visible[None], score, masked_score)
        peak = jnp.max(score, axis=-1)
        weights = jnp.where(visible[None], jnp.exp(score - peak[..., None]), 0.0)
        total = jnp.sum(weights, axis=-1)
        context = jnp.einsum(
            "gqk,kd->qgd",
            weights.astype(jnp.bfloat16),
            value_block,
            preferred_element_type=jnp.float32,
        )
        divisor = jnp.transpose(jnp.maximum(total, 1.0))[:, :, None]
        return ((context / divisor).astype(jnp.bfloat16), peak, total)

    outputs, peaks, totals = lax.map(attend, (query_heads, key_heads, value_heads))
    block_output = jnp.transpose(outputs, (1, 0, 2, 3)).reshape(appended, width)
    peaks = peaks.reshape(H, appended)
    totals = totals.reshape(H, appended)
    peak_blocks, total_blocks = (
        lax.all_gather(peaks[None], "kv", axis=0, tiled=True),
        lax.all_gather(totals[None], "kv", axis=0, tiled=True),
    )
    peak_all = jnp.max(peak_blocks, axis=0)
    share = jnp.exp(peak_blocks - peak_all[None]) * total_blocks
    received = lax.all_to_all(block_output, "kv", split_axis=0, concat_axis=0, tiled=True)
    blocks_here = received.reshape(kv_count, rows_here, width)
    share_here = lax.dynamic_slice_in_dim(share, kv_index * rows_here, rows_here, 2)
    context_here = combine_blocks(blocks_here, share_here)
    out_cols = lax.all_gather(w_out, "kv", axis=1, tiled=True)
    result = fold_single(context_here, lax.all_gather(out_cols, "req", axis=0, tiled=True))
    return (result.astype(jnp.bfloat16)[None], new_keys[None], new_values[None])


def solution(mesh):
    return jax.shard_map(
        body,
        mesh=mesh,
        in_specs=(
            P("req", "kv", None),
            P("req"),
            P("req", "kv", None),
            P("req", "kv", None),
            P(),
            P("req", "kv"),
            P("req", "kv"),
            P("req", "kv"),
            P("req", "kv"),
        ),
        out_specs=(P("req", "kv", None), P("req", "kv", None), P("req", "kv", None)),
        check_vma=False,
    )
```

profile of v0, /device:TPU:16, one launch (start us, length us, event | category | flops | bytes accessed | tf_op | source)
XLA Modules:
  0.0 1278.3 jit_solution(5281821043887652498)
XLA Ops:
  7.2 7.5 all_gather.37
  14.8 7.0 all-gather.1
  22.6 6.9 all-gather
  33.4 290.6 %all-gather.12.cloned.1.call-done = bf16[1536,1536]{1,0:T(8,128)(2,1)} async-done(((bf16[24,1536]{1,0:T(8,128)(2,1)}), bf16[1536,1536]{1,0:T(8,128)(2,1)}) %all-gather.12.cloned.1.call-update) | async-done | bytes 4718608 | tf_op jit(solution)/shard_map/all_gather | solution.py:76
  323.9 6.8 copy.49
  330.7 3.9 fusion.50
  335.9 7.5 all_gather.42
  344.7 279.0 %all-gather.10.cloned.1.call-done = bf16[1536,768]{1,0:T(8,128)(2,1)} async-done(((bf16[24,768]{1,0:T(8,128)(2,1)}), bf16[1536,768]{1,0:T(8,128)(2,1)}) %all-gather.10.cloned.1.call-update) | async-done | bytes 2359312 | tf_op jit(solution)/shard_map/all_gather | solution.py:77
  623.6 4.4 copy.48
  628.0 2.6 fusion.52
  631.5 292.6 %all-gather.8.cloned.1.call-done = bf16[1536,768]{1,0:T(8,128)(2,1)} async-done(((bf16[24,768]{1,0:T(8,128)(2,1)}), bf16[1536,768]{1,0:T(8,128)(2,1)}) %all-gather.8.cloned.1.call-update) | async-done | bytes 2359312 | tf_op jit(solution)/shard_map/all_gather | solution.py:78
  930.0 26.4 %all-gather.14.cloned.1.call-done = bf16[1024,1536]{0,1:T(8,128)(2,1)} async-done(((bf16[256,1536]{0,1:T(8,128)(2,1)}), bf16[1024,1536]{0,1:T(8,128)(2,1)}) %all-gather.14.cloned.1.call-update) | async-done | bytes 3145744 | tf_op jit(solution)/shard_map/all_gather | solution.py:87
  956.4 69.6 %while.14 = (s32[]{:T(128)}, bf16[8,1024,2,96]{1,3,2,0:T(8,128)(2,1)}, f32[8,2,1024]{2,1,0:T(2,128)}, f32[8,2,1024]{2,1,0:T(2,128)}, bf16[8,768,96]{1,2,0:T(8,12...) while((s32[]{:T(128)}, ...), condition=%wide.region_4.5_spmd, body=%wide.region_1.4_spmd.sunk | while | flops 624818176 | bytes 22407772 | solution.py:124
  961.2 3.9 fusion.70
  965.1 2.6 fusion.68
  970.0 3.9 fusion.70
  978.7 3.9 fusion.70
  982.6 2.6 fusion.68
  987.4 3.9 fusion.70
  991.3 2.6 fusion.68
  996.1 3.9 fusion.70
  1000.0 2.6 fusion.68
  1004.8 3.9 fusion.70
  1013.5 3.9 fusion.70
  1017.4 2.6 fusion.68
  1022.2 3.9 fusion.70
  1026.1 4.8 all_to_all.6
  1032.9 6.9 all-to-all-start
  1042.6 55.7 %all_gather.40 = f32[4,16,1024]{2,1,0:T(8,128)S(1)} all-gather(f32[1,16,1024]{2,1,0:T(8,128)S(1)} %broadcast_in_dim_reshape.6), channel_id=1, replica_groups=mesh['req'=64,'kv'=4] {'kv'}, dimensions={0}, use_global_device_ids=true | all-gather | bytes 327680 | tf_op jit(solution)/shard_map/all_gather | solution.py:129
  1098.2 8.7 all_gather.41
  1108.6 158.3 %all-gather.16.cloned.1.call-done = bf16[1536,1536]{1,0:T(8,128)(2,1)} async-done(((bf16[24,1536]{1,0:T(8,128)(2,1)}), bf16[1536,1536]{1,0:T(8,128)(2,1)}) %all-gather.16.cloned.1.call-update) | async-done | bytes 4718608 | tf_op jit(solution)/shard_map/all_gather | solution.py:139
  1266.9 4.9 fusion.33
  (94 shorter events, 45.4 us)
Async XLA Ops:
  7.2 316.8 %all-gather.12.cloned.1.call-start = ((), (), s32[]{:S(2)}) async-start(), calls=%async_computation.3 | async-start | bytes 4792320 | tf_op jit(solution)/shard_map/all_gather | solution.py:76
  14.8 608.9 %all-gather.10.cloned.1.call-start = ((), (), s32[]{:S(2)}) async-start(), calls=%async_computation.2 | async-start | bytes 2396160 | tf_op jit(solution)/shard_map/all_gather | solution.py:77
  22.5 901.5 %all-gather.8.cloned.1.call-start = ((), (), s32[]{:S(2)}) async-start(), calls=%async_computation.1 | async-start | bytes 2396160 | tf_op jit(solution)/shard_map/all_gather | solution.py:78
  30.3 926.1 %all-gather.14.cloned.1.call-start = ((), (), s32[]{:S(2)}) async-start(), calls=%async_computation.4 | async-start | bytes 3932160 | tf_op jit(solution)/shard_map/all_gather | solution.py:87
  33.3 301.2 %copy-start.4 = (f32[256,48]{0,1:T(8,128)}, f32[256,48]{0,1:T(8,128)S(1)}, u32[]{:S(2)}) copy-start(f32[256,48]{0,1:T(8,128)S(1)} %get-tuple-element.92) | copy-start | bytes 147460
  33.3 301.2 %copy-start.6 = (f32[256,48]{0,1:T(8,128)}, f32[256,48]{0,1:T(8,128)S(1)}, u32[]{:S(2)}) copy-start(f32[256,48]{0,1:T(8,128)S(1)} %get-tuple-element.93) | copy-start | bytes 147460
  323.9 6.8 copy-start.2
  334.6 1.3 copy-start.9
  334.6 8.9 copy-start
  334.9 8.9 copy-start.1
  335.9 931.0 %all-gather.16.cloned.1.call-start = ((), (), s32[]{:S(2)}) async-start(), calls=%async_computation.5 | async-start | bytes 4792320 | tf_op jit(solution)/shard_map/all_gather | solution.py:139
  623.6 4.4 copy-start.3
  628.0 2.6 copy-start.5
  628.0 2.6 copy-start.7
  926.5 0.7 copy-start.8
  1032.9 74.1 %all-to-all-start = ((bf16[4,256,1536]{1,2,0:T(8,128)(2,1)}), bf16[4,256,1536]{1,2,0:T(8,128)(2,1)S(1)}, u32[]{:S(2)}, u32[]{:S(2)}) async-start(bf16[4,256,1536]{1,2,0:T(8,128)(2,1)} %copy.50), calls=%async_computation | async-start | bytes 6291456 | tf_op jit(solution)/shard_map/all_to_all | solution.py:134
Sparse Core Ops, SparseCore 0:
  14.9 308.9 all-gather.11
  325.7 297.8 all-gather.9
  625.4 298.5 all-gather.7
  926.2 30.1 all-gather.13
  958.1 308.7 all-gather.15
where the time goes:
time: 1280 us
  waiting for transfers between devices  1050 us (82%)
  blocking collectives  93.3 us (7%)
  matrix products  65.2 us (5%)
  local copies, waits for them, and re-layouts  28.3 us (2%)
  other arithmetic  22.5 us (2%)
  between operations  14.7 us (1%)
    all_gather x1, waiting for transfers between devices, body(): lax.all_gather(value_cols, 'req', axis=0, tiled=True)  293 us
    all_gather x1, waiting for transfers between devices, body(): lax.all_gather(query_cols, 'req', axis=0, tiled=True)  291 us
    all_gather x1, waiting for transfers between devices, body(): lax.all_gather(key_cols, 'req', axis=0, tiled=True)  279 us
    all_gather x1, waiting for transfers between devices, body(): lax.all_gather(out_cols, 'req', axis=0, tiled=True)  158 us
    all_gather x1, blocking collectives, body(): lax.all_gather(peaks[None], 'kv', axis=0, tiled=True)  55.7 us
    dot_general x8, matrix products, attend(): jnp.einsum('gqk,kd->qgd', weights.astype(jnp.bfloat16), value_block, pref...  31 us
    all_gather x1, waiting for transfers between devices, body(): queries = lax.all_gather(queries_here, 'kv', axis=0, tiled=True)  26.4 us
  transfers between devices with their start and end apart: 6, of which 5 were waited for; matrix products, arithmetic and copies ran while one was open for 8% of the time, Pallas kernels for 0%

commit v1 on v0

--- a/solution.py
+++ b/solution.py
@@ -73,7 +73,9 @@
     proj_query, proj_key, proj_value = fold_three(
         normed,
         (
-            lax.all_gather(query_cols, "req", axis=0, tiled=True),
+            jnp.concatenate(
+                lax.all_to_all(jnp.stack([query_cols] * lax.axis_size("req")), "req", 0, 0), axis=0
+            ),
             lax.all_gather(key_cols, "req", axis=0, tiled=True),
             lax.all_gather(value_cols, "req", axis=0, tiled=True),
         ),

time: 1280 us -> 1010 us (0.79)
  waiting for transfers between devices: 1050 us -> 762 us
  starting transfers between devices: 7.15 us -> 20.1 us
    all_gather x1 -> x0, waiting for transfers between devices: 291 us -> none  [body(): lax.all_gather(query_cols, 'req', axis=0, tiled=True)]
    all_to_all x0 -> x1, waiting for transfers between devices: none -> 93.2 us  [body(): lax.all_to_all(jnp.stack([query_cols] * lax.axis_size('req')), 'req', 0, 0)]
    all_gather x1, waiting for transfers between devices: 279 us -> 190 us  [body(): lax.all_gather(key_cols, 'req', axis=0, tiled=True)]
    all_to_all x0 -> x1, starting transfers between devices: none -> 13 us  [body(): lax.all_to_all(jnp.stack([query_cols] * lax.axis_size('req')), 'req', 0, 0)]
  transfers between devices with their start and end apart: 6 -> 6, of which waited for: 5 -> 5; matrix products, arithmetic and copies ran while one was open for 8% -> 10% of each run, Pallas kernels for 0% -> 0%
where the time goes in v1:
time: 1010 us
  waiting for transfers between devices  762 us (75%)
  blocking collectives  97.8 us (10%)
  matrix products  65.3 us (6%)
  local copies, waits for them, and re-layouts  30.7 us (3%)
  other arithmetic  20.7 us (2%)
  starting transfers between devices  20.1 us (2%)
  between operations  14.8 us (1%)
    all_gather x1, waiting for transfers between devices, body(): lax.all_gather(value_cols, 'req', axis=0, tiled=True)  293 us
    all_gather x1, waiting for transfers between devices, body(): lax.all_gather(key_cols, 'req', axis=0, tiled=True)  190 us
    all_gather x1, waiting for transfers between devices, body(): lax.all_gather(out_cols, 'req', axis=0, tiled=True)  159 us
    all_to_all x1, waiting for transfers between devices, body(): lax.all_to_all(jnp.stack([query_cols] * lax.axis_size('req')), 'req', 0, 0)  93.2 us
    all_gather x1, blocking collectives, body(): lax.all_gather(peaks[None], 'kv', axis=0, tiled=True)  55.6 us
    dot_general x8, matrix products, attend(): jnp.einsum('gqk,kd->qgd', weights.astype(jnp.bfloat16), value_block, pref...  31 us
    all_gather x1, waiting for transfers between devices, body(): queries = lax.all_gather(queries_here, 'kv', axis=0, tiled=True)  26.6 us
    dot_general x8, matrix products, attend(): jnp.einsum('qgd,kd->gqk', query_block, key_block, preferred_element_type=...  20.5 us
  transfers between devices with their start and end apart: 6, of which 5 were waited for; matrix products, arithmetic and copies ran while one was open for 10% of the time, Pallas kernels for 0%

profile of v1, /device:TPU:16, one launch (start us, length us, event | category | flops | bytes accessed | tf_op | source)
XLA Modules:
  0.0 1011.4 jit_solution(17686261308464075647)
XLA Ops:
  7.2 7.0 all_gather.34
  16.7 13.0 %all-to-all-start = ((bf16[64,24,1536]{2,1,0:T(8,128)(2,1)}), bf16[64,24,1536]{2,1,0:T(8,128)(2,1)}, u32[]{:S(2)}, u32[]{:S(2)}) async-start(bf16[64,24,1536]{2,1,0:T(8,128)(2,1)} %stack.2), calls=%async_computation | async-start | bytes 9437184 | tf_op jit(solution)/shard_map/all_to_all | solution.py:77
  29.8 12.4 %all-gather.1 = bf16[4,192,24]{1,2,0:T(8,128)(2,1)S(1)} all-gather(bf16[1,192,24]{1,2,0:T(8,128)(2,1)S(1)} %bitcast.199), channel_id=1, replica_groups=mesh['req'=64,'kv'=4] {'kv'}, dimensions={0}, use_global_device_ids=true | all-gather | bytes 46080 | tf_op jit(solution)/shard_map/all_gather | solution.py:70
  43.0 6.8 all-gather
  51.9 93.2 %all-to-all-done = bf16[64,24,1536]{2,1,0:T(8,128)(2,1)} async-done(((bf16[64,24,1536]{2,1,0:T(8,128)(2,1)}), bf16[64,24,1536]{2,1,0:T(8,128)(2,1)}, u32[]{:S(2)}, u32[]{:S(2)}) %all-to-all-start) | async-done | bytes 4718624 | tf_op jit(solution)/shard_map/all_to_all | solution.py:77
  145.1 6.7 copy.49
  151.7 3.9 fusion.50
  156.9 7.5 all_gather.38
  165.7 190.4 %all-gather.9.cloned.1.call-done = bf16[1536,768]{1,0:T(8,128)(2,1)} async-done(((bf16[24,768]{1,0:T(8,128)(2,1)}), bf16[1536,768]{1,0:T(8,128)(2,1)}) %all-gather.9.cloned.1.call-update) | async-done | bytes 2359312 | tf_op jit(solution)/shard_map/all_gather | solution.py:79
  356.1 4.4 copy.48
  360.5 2.6 fusion.52
  363.9 292.9 %all-gather.7.cloned.1.call-done = bf16[1536,768]{1,0:T(8,128)(2,1)} async-done(((bf16[24,768]{1,0:T(8,128)(2,1)}), bf16[1536,768]{1,0:T(8,128)(2,1)}) %all-gather.7.cloned.1.call-update) | async-done | bytes 2359312 | tf_op jit(solution)/shard_map/all_gather | solution.py:80
  662.8 26.6 %all-gather.11.cloned.1.call-done = bf16[1024,1536]{0,1:T(8,128)(2,1)} async-done(((bf16[256,1536]{0,1:T(8,128)(2,1)}), bf16[1024,1536]{0,1:T(8,128)(2,1)}) %all-gather.11.cloned.1.call-update) | async-done | bytes 3145744 | tf_op jit(solution)/shard_map/all_gather | solution.py:89
  689.4 69.6 %while.14 = (s32[]{:T(128)}, bf16[8,1024,2,96]{1,3,2,0:T(8,128)(2,1)}, f32[8,2,1024]{2,1,0:T(2,128)}, f32[8,2,1024]{2,1,0:T(2,128)}, bf16[8,768,96]{1,2,0:T(8,12...) while((s32[]{:T(128)}, ...), condition=%wide.region_4.5_spmd, body=%wide.region_1.4_spmd.sunk | while | flops 624818176 | bytes 22407772 | solution.py:126
  694.2 3.9 fusion.70
  703.0 3.9 fusion.70
  711.7 3.9 fusion.70
  715.6 2.6 fusion.68
  720.4 3.9 fusion.70
  724.3 2.6 fusion.68
  729.1 3.9 fusion.70
  733.0 2.6 fusion.68
  737.8 3.9 fusion.70
  746.5 3.9 fusion.70
  750.3 2.6 fusion.68
  755.2 3.9 fusion.70
  759.0 4.8 all_to_all.10
  765.9 6.9 all-to-all-start.1
  775.5 55.6 %all_gather.36 = f32[4,16,1024]{2,1,0:T(8,128)S(1)} all-gather(f32[1,16,1024]{2,1,0:T(8,128)S(1)} %broadcast_in_dim_reshape.6), channel_id=1, replica_groups=mesh['req'=64,'kv'=4] {'kv'}, dimensions={0}, use_global_device_ids=true | all-gather | bytes 327680 | tf_op jit(solution)/shard_map/all_gather | solution.py:131
  831.1 8.5 all_gather.37
  841.2 158.8 %all-gather.13.cloned.1.call-done = bf16[1536,1536]{1,0:T(8,128)(2,1)} async-done(((bf16[24,1536]{1,0:T(8,128)(2,1)}), bf16[1536,1536]{1,0:T(8,128)(2,1)}) %all-gather.13.cloned.1.call-update) | async-done | bytes 4718608 | tf_op jit(solution)/shard_map/all_gather | solution.py:141
  1000.0 4.9 fusion.33
  (100 shorter events, 48.6 us)
Async XLA Ops:
  16.7 13.1 %copy-start.10 = (bf16[24,192]{1,0:T(8,128)(2,1)S(1)}, bf16[24,192]{1,0:T(8,128)(2,1)}, u32[]{:S(2)}) copy-start(bf16[24,192]{1,0:T(8,128)(2,1)} %param.17) | copy-start | bytes 27652
  16.7 26.4 %copy-start.11 = (bf16[24,192]{1,0:T(8,128)(2,1)S(1)}, bf16[24,192]{1,0:T(8,128)(2,1)}, u32[]{:S(2)}) copy-start(bf16[24,192]{1,0:T(8,128)(2,1)} %param.18) | copy-start | bytes 27652
  16.7 34.6 %copy-start.12 = (bf16[1536]{0:T(1024)(128)(2,1)S(1)}, bf16[1536]{0:T(1024)(128)(2,1)}, u32[]{:S(2)}) copy-start(bf16[1536]{0:T(1024)(128)(2,1)} %param.15) | copy-start | bytes 9220
  16.7 34.7 %copy-start.2 = (bf16[1,256,1536]{2,1,0:T(8,128)(2,1)S(1)}, bf16[1,256,1536]{2,1,0:T(8,128)(2,1)}, u32[]{:S(2)}) copy-start(bf16[1,256,1536]{2,1,0:T(8,128)(2,1)} %param.11) | copy-start | bytes 2359300
  16.7 128.4 %all-to-all-start = ((bf16[64,24,1536]{2,1,0:T(8,128)(2,1)}), bf16[64,24,1536]{2,1,0:T(8,128)(2,1)}, u32[]{:S(2)}, u32[]{:S(2)}) async-start(bf16[64,24,1536]{2,1,0:T(8,128)(2,1)} %stack.2), calls=%async_computation | async-start | bytes 9437184 | tf_op jit(solution)/shard_map/all_to_all | solution.py:77
  29.7 326.4 %all-gather.9.cloned.1.call-start = ((), (), s32[]{:S(2)}) async-start(), calls=%async_computation.3 | async-start | bytes 2396160 | tf_op jit(solution)/shard_map/all_gather | solution.py:79
  43.0 613.9 %all-gather.7.cloned.1.call-start = ((), (), s32[]{:S(2)}) async-start(), calls=%async_computation.2 | async-start | bytes 2396160 | tf_op jit(solution)/shard_map/all_gather | solution.py:80
  50.6 638.8 %all-gather.11.cloned.1.call-start = ((), (), s32[]{:S(2)}) async-start(), calls=%async_computation.4 | async-start | bytes 3932160 | tf_op jit(solution)/shard_map/all_gather | solution.py:89
  51.9 103.7 %copy-start.4 = (f32[256,48]{0,1:T(8,128)}, f32[256,48]{0,1:T(8,128)S(1)}, u32[]{:S(2)}) copy-start(f32[256,48]{0,1:T(8,128)S(1)} %get-tuple-element.92) | copy-start | bytes 147460
  51.9 103.7 %copy-start.6 = (f32[256,48]{0,1:T(8,128)}, f32[256,48]{0,1:T(8,128)S(1)}, u32[]{:S(2)}) copy-start(f32[256,48]{0,1:T(8,128)S(1)} %get-tuple-element.93) | copy-start | bytes 147460
  155.6 1.3 copy-start.9
  155.6 8.9 copy-start
  155.9 8.9 copy-start.1
  156.9 843.1 %all-gather.13.cloned.1.call-start = ((), (), s32[]{:S(2)}) async-start(), calls=%async_computation.5 | async-start | bytes 4792320 | tf_op jit(solution)/shard_map/all_gather | solution.py:141
  356.1 4.4 copy-start.3
  360.4 2.6 copy-start.5
  360.5 2.6 copy-start.7
  659.3 0.7 copy-start.8
  765.9 73.7 %all-to-all-start.1 = ((bf16[4,256,1536]{1,2,0:T(8,128)(2,1)}), bf16[4,256,1536]{1,2,0:T(8,128)(2,1)S(1)}, u32[]{:S(2)}, u32[]{:S(2)}) async-start(bf16[4,256,1536]{1,2,0:T(8,128)(2,1)} %copy.50), calls=%async_computation.1 | async-start | bytes 6291456 | tf_op jit(solution)/shard_map/all_to_all | solution.py:136
Sparse Core Ops, SparseCore 0:
  43.1 312.9 all-gather.8
  357.9 298.9 all-gather.6
  659.2 30.1 all-gather.10
  691.0 308.9 all-gather.12
